TPU v7x, 32 devices: a whole 2x2x4 slice. The times are simulated.
32 devices in a mesh: tensor: 2 (over y), dp: 16 (over z, x, core).
Axes of the slice: x: 2, y: 2, z: 4, core: 2. Of those that a mesh axis runs over, the one named last changes fastest.
Arguments:
- inputs: bfloat16 [2, 4096, 768], P(None, 'dp'), may hold values from -6 to 6
- cotangent: bfloat16 [2, 4096, 768], P(None, 'dp'), may hold values from -6 to 6
- segments: int32 [2, 4096], replicated, may hold values from 0 to 31, never falling along the last dimension, each value on 1 to 512 neighbouring positions
- qkv_weight: float32 [768, 3, 768], P('dp', None, 'tensor'), may hold values from -0.21875 to 0.21875
- out_weight: float32 [768, 768], P('dp', 'tensor'), may hold values from -0.875 to 0.875
- gateup_weight: float32 [768, 2, 3072], P('dp', None, 'tensor'), may hold values from -0.21875 to 0.21875
- down_weight: float32 [768, 3072], P('dp', 'tensor'), may hold values from -0.21875 to 0.21875
- norm_gains: float32 [768, 2], P('dp'), may hold values from 0.5 to 1.5
- qkv_momentum: float32 [768, 3, 768], P('dp', None, 'tensor'), may hold values from -64 to 64
- out_momentum: float32 [768, 768], P('dp', 'tensor'), may hold values from -64 to 64
- gateup_momentum: float32 [768, 2, 3072], P('dp', None, 'tensor'), may hold values from -64 to 64
- down_momentum: float32 [768, 3072], P('dp', 'tensor'), may hold values from -64 to 64
- gains_momentum: float32 [768, 2], P('dp'), may hold values from -64 to 64
- qkv_average: float32 [768, 3, 768], P('dp', None, 'tensor'), may hold values from -0.21875 to 0.21875
- out_average: float32 [768, 768], P('dp', 'tensor'), may hold values from -0.875 to 0.875
- gateup_average: float32 [768, 2, 3072], P('dp', None, 'tensor'), may hold values from -0.21875 to 0.21875
- down_average: float32 [768, 3072], P('dp', 'tensor'), may hold values from -0.21875 to 0.21875
- gains_average: float32 [768, 2], P('dp'), may hold values from -0.5 to 0.5
Outputs:
- output: bfloat16 [2, 4096, 768], P(None, 'dp')
- input_grad: float32 [2, 4096, 768], P(None, 'dp')
- qkv_grad: float32 [768, 3, 768], P('dp', None, 'tensor')
- out_grad: float32 [768, 768], P('dp', 'tensor')
- gateup_grad: float32 [768, 2, 3072], P('dp', None, 'tensor')
- down_grad: float32 [768, 3072], P('dp', 'tensor')
- gains_grad: float32 [768, 2], P('dp')
- qkv_moment: float32 [768, 3, 768], P('dp', None, 'tensor')
- out_moment: float32 [768, 768], P('dp', 'tensor')
- gateup_moment: float32 [768, 2, 3072], P('dp', None, 'tensor')
- down_moment: float32 [768, 3072], P('dp', 'tensor')
- gains_moment: float32 [768, 2], P('dp')
- qkv_updated: float32 [768, 3, 768], P('dp', None, 'tensor')
- out_updated: float32 [768, 768], P('dp', 'tensor')
- gateup_updated: float32 [768, 2, 3072], P('dp', None, 'tensor')
- down_updated: float32 [768, 3072], P('dp', 'tensor')
- gains_updated: float32 [768, 2], P('dp')
- qkv_averaged: float32 [768, 3, 768], P('dp', None, 'tensor')
- out_averaged: float32 [768, 768], P('dp', 'tensor')
- gateup_averaged: float32 [768, 2, 3072], P('dp', None, 'tensor')
- down_averaged: float32 [768, 3072], P('dp', 'tensor')
- gains_averaged: float32 [768, 2], P('dp')
Inputs may be any that keep to these rules, and one draw needn't show every extreme that they name: `segments`: along each sequence the document numbers never fall; every document has 1 to 512 tokens and one document of each sequence has exactly 512.
All inputs are finite; a program needn't handle non-finite values.
Results may differ from a plain program's by a relative error of at most 0.015.
The roundings to bfloat16 on the way count: a program that leaves them out, or rounds other values in their place, can miss the bound.
Values may be sent and summed in bfloat16 or wider, within the bound.
No kernel may reach another device: no remote copies, remote signals or barrier semaphores. Data moves between devices by JAX's collectives and lax.ppermute only.
A program may use at most 128 MiB of HBM per device.

v0:
```python
import jax
import jax.numpy as jnp
from jax import lax
from jax.sharding import PartitionSpec as P

HEAD_DIM = 64
REACH = 2
NORM_EPS = 1e-05
ROPE_BASE = 10000.0
MOMENTUM = 0.9
LEARN_RATE = 0.0003
AVERAGE_RATE = 0.9
MASKED = -1e30


def from_behind(value, axis, steps):
    count = lax.axis_size(axis)
    initial, last = (max(0, -steps), min(count, count - steps))
    return lax.ppermute(value, axis, [(source, source + steps) for source in range(initial, last)])


def rotate_half(values):
    half = values.shape[-1] // 2
    return jnp.concatenate([-values[..., half:], values[..., :half]], axis=-1)


def rope_tables(first, count):
    position = (first + jnp.arange(count, dtype=jnp.int32)).astype(jnp.float32)
    inverse = ROPE_BASE ** (-jnp.arange(0, HEAD_DIM, 2, dtype=jnp.float32) / HEAD_DIM)
    angles = position[:, None] * inverse[None, :]
    angles = jnp.concatenate([angles, angles], axis=-1)
    return (jnp.cos(angles)[:, None, :], jnp.sin(angles)[:, None, :])


def apply_rope(values, cosine, sine):
    return values * cosine + rotate_half(values) * sine


def undo_rope(gradient, cosine, sine):
    return gradient * cosine - rotate_half(gradient * sine)


def norm_forward(values, gain):
    scale_inv = lax.rsqrt(jnp.mean(values * values, axis=-1, keepdims=True) + NORM_EPS)
    unit = values * scale_inv
    return (scale_inv, unit, (unit * gain).astype(jnp.bfloat16))


def norm_backward(scale_inv, unit, gain, upstream):
    weighted = upstream * gain
    inner = jnp.mean(weighted * unit, axis=-1, keepdims=True)
    return (scale_inv * (weighted - unit * inner), jnp.sum(unit * upstream, axis=0))


def scores_of(queries, keys_all, visible):
    raw = jnp.einsum("qhe,khe->hqk", queries, keys_all, preferred_element_type=jnp.float32)
    return jnp.where(visible[None], raw * HEAD_DIM ** (-0.5), MASKED)


def micro_step(tokens, upstream, seg_row, whole, rank):
    qkv_full, out_full, gateup_full, down_full, gains_full = whole
    gain_one = gains_full[:, 0].astype(jnp.float32)
    gain_two = gains_full[:, 1].astype(jnp.float32)
    count = tokens.shape[0]
    width = qkv_full.shape[2]
    heads = width // HEAD_DIM
    span = (REACH + 1) * count
    start = rank * count
    scale = HEAD_DIM ** (-0.5)
    tokens_wide = tokens.astype(jnp.float32)
    scale_one, unit_one, normed_one = norm_forward(tokens_wide, gain_one)
    mixed = jnp.einsum("td,dch->tch", normed_one, qkv_full, preferred_element_type=jnp.float32)
    cosine, sine = rope_tables(start, count)
    queries = apply_rope(mixed[:, 0].reshape(count, heads, HEAD_DIM), cosine, sine).astype(
        jnp.bfloat16
    )
    keys_own = apply_rope(mixed[:, 1].reshape(count, heads, HEAD_DIM), cosine, sine).astype(
        jnp.bfloat16
    )
    values_own = mixed[:, 2].reshape(count, heads, HEAD_DIM).astype(jnp.bfloat16)
    earlier = []
    for hop in range(REACH, 0, -1):
        earlier.append(from_behind((keys_own, values_own), "dp", hop))
    keys_all = jnp.concatenate([received[0] for received in earlier] + [keys_own], axis=0)
    values_all = jnp.concatenate([received[1] for received in earlier] + [values_own], axis=0)
    padded = jnp.concatenate([jnp.full((REACH * count,), -1, jnp.int32), seg_row])
    seg_keys = lax.dynamic_slice_in_dim(padded, start, span)
    seg_query = lax.dynamic_slice_in_dim(seg_row, start, count)
    query_pos = jnp.arange(count, dtype=jnp.int32)[:, None] + REACH * count
    key_pos = jnp.arange(span, dtype=jnp.int32)[None, :]
    visible = (seg_query[:, None] == seg_keys[None, :]) & (key_pos <= query_pos)
    scores = scores_of(queries, keys_all, visible)
    peak = jnp.max(scores, axis=-1, keepdims=True)
    expon = jnp.exp(scores - peak)
    totals = jnp.sum(expon, axis=-1, keepdims=True)
    log_total = peak + jnp.log(totals)
    probs_low = (expon / totals).astype(jnp.bfloat16)
    attended = jnp.einsum("hqk,khe->qhe", probs_low, values_all, preferred_element_type=jnp.float32)
    attended = attended.reshape(count, width).astype(jnp.bfloat16)
    branch = jnp.einsum("th,dh->td", attended, out_full, preferred_element_type=jnp.float32)
    branch = lax.psum(branch, "tensor")
    resid = tokens_wide + branch
    scale_two, unit_two, normed_two = norm_forward(resid, gain_two)
    gateup = jnp.einsum("td,dcf->tcf", normed_two, gateup_full, preferred_element_type=jnp.float32)
    gate = gateup[:, 0]
    upward = gateup[:, 1]
    sigma = jax.nn.sigmoid(gate)
    active = gate * sigma
    hidden = (active * upward).astype(jnp.bfloat16)
    down_part = jnp.einsum("tf,df->td", hidden, down_full, preferred_element_type=jnp.float32)
    down_part = lax.psum(down_part.astype(jnp.bfloat16), "tensor").astype(jnp.float32)
    result = (resid + down_part).astype(jnp.bfloat16)
    grad_hidden = jnp.einsum("td,df->tf", upstream, down_full, preferred_element_type=jnp.float32)
    down_grad = jnp.einsum("td,tf->df", upstream, hidden, preferred_element_type=jnp.float32)
    grad_gate = grad_hidden * upward * sigma * (1.0 + gate * (1.0 - sigma))
    grad_up = grad_hidden * active
    grad_gateup = jnp.stack([grad_gate, grad_up], axis=1).astype(jnp.bfloat16)
    gateup_grad = jnp.einsum(
        "td,tcf->dcf", normed_two, grad_gateup, preferred_element_type=jnp.float32
    )
    grad_normed_two = jnp.einsum(
        "tcf,dcf->td", grad_gateup, gateup_full, preferred_element_type=jnp.float32
    )
    grad_normed_two = lax.psum(grad_normed_two, "tensor")
    grad_resid_norm, gain_two_grad = norm_backward(scale_two, unit_two, gain_two, grad_normed_two)
    grad_resid = upstream.astype(jnp.float32) + grad_resid_norm
    grad_branch = grad_resid.astype(jnp.bfloat16)
    grad_attended = jnp.einsum(
        "td,dh->th", grad_branch, out_full, preferred_element_type=jnp.float32
    ).astype(jnp.bfloat16)
    out_grad = jnp.einsum("td,th->dh", grad_branch, attended, preferred_element_type=jnp.float32)
    grad_heads = grad_attended.reshape(count, heads, HEAD_DIM)
    scores = scores_of(queries, keys_all, visible)
    probs = jnp.exp(scores - log_total)
    probs_back = probs.astype(jnp.bfloat16)
    grad_probs = jnp.einsum(
        "qhe,khe->hqk", grad_heads, values_all, preferred_element_type=jnp.float32
    )
    inner = jnp.sum(probs * grad_probs, axis=-1, keepdims=True)
    grad_scores = (probs * (grad_probs - inner)).astype(jnp.bfloat16)
    grad_queries = (
        jnp.einsum("hqk,khe->qhe", grad_scores, keys_all, preferred_element_type=jnp.float32)
        * scale
    )
    grad_keys = (
        jnp.einsum("hqk,qhe->khe", grad_scores, queries, preferred_element_type=jnp.float32) * scale
    )
    grad_values = jnp.einsum(
        "hqk,qhe->khe", probs_back, grad_heads, preferred_element_type=jnp.float32
    )
    own_keys = grad_keys[REACH * count :]
    own_values = grad_values[REACH * count :]
    for hop in range(1, REACH + 1):
        first = (REACH - hop) * count
        returned = (
            from_behind(grad_keys[first : first + count].astype(jnp.bfloat16), "dp", -hop).astype(
                jnp.float32
            ),
            from_behind(grad_values[first : first + count].astype(jnp.bfloat16), "dp", -hop).astype(
                jnp.float32
            ),
        )
        own_keys = own_keys + returned[0]
        own_values = own_values + returned[1]
    grad_q = undo_rope(grad_queries, cosine, sine).reshape(count, width)
    grad_k = undo_rope(own_keys, cosine, sine).reshape(count, width)
    grad_v = own_values.reshape(count, width)
    grad_mixed = jnp.stack([grad_q, grad_k, grad_v], axis=1).astype(jnp.bfloat16)
    qkv_grad = jnp.einsum("td,tch->dch", normed_one, grad_mixed, preferred_element_type=jnp.float32)
    grad_normed_one = jnp.einsum(
        "tch,dch->td", grad_mixed, qkv_full, preferred_element_type=jnp.float32
    )
    grad_normed_one = lax.psum(grad_normed_one, "tensor")
    grad_tokens_norm, gain_one_grad = norm_backward(scale_one, unit_one, gain_one, grad_normed_one)
    grad_tokens = grad_resid + grad_tokens_norm
    gains_grad = jnp.stack([gain_one_grad, gain_two_grad], axis=1)
    return (result, grad_tokens, (qkv_grad, out_grad, gateup_grad, down_grad, gains_grad))


def body(
    inputs,
    cotangent,
    segments,
    qkv_weight,
    out_weight,
    gateup_weight,
    down_weight,
    norm_gains,
    qkv_momentum,
    out_momentum,
    gateup_momentum,
    down_momentum,
    gains_momentum,
    qkv_average,
    out_average,
    gateup_average,
    down_average,
    gains_average,
):
    masters = (qkv_weight, out_weight, gateup_weight, down_weight, norm_gains)
    shards = tuple((master.astype(jnp.bfloat16) for master in masters))
    rank = lax.axis_index("dp")
    totals = tuple((jnp.zeros(master.shape, jnp.float32) for master in masters))
    results = []
    input_grads = []
    for index in range(inputs.shape[0]):
        whole = (
            lax.all_gather(shards[0], "dp", axis=0, tiled=True),
            lax.all_gather(shards[1], "dp", axis=0, tiled=True),
            lax.all_gather(shards[2], "dp", axis=0, tiled=True),
            lax.all_gather(shards[3], "dp", axis=0, tiled=True),
            lax.all_gather(shards[4], "dp", axis=0, tiled=True),
        )
        result, grad_tokens, local_grads = micro_step(
            inputs[index], cotangent[index], segments[index], whole, rank
        )
        shared = (
            lax.psum_scatter(local_grads[0], "dp", scatter_dimension=0, tiled=True),
            lax.psum_scatter(local_grads[1], "dp", scatter_dimension=0, tiled=True),
            lax.psum_scatter(local_grads[2], "dp", scatter_dimension=0, tiled=True),
            lax.psum_scatter(local_grads[3], "dp", scatter_dimension=0, tiled=True),
            lax.psum_scatter(local_grads[4], "dp", scatter_dimension=0, tiled=True),
        )
        totals = tuple((total + piece for total, piece in zip(totals, shared)))
        results.append(result)
        input_grads.append(grad_tokens)
    moments = (qkv_momentum, out_momentum, gateup_momentum, down_momentum, gains_momentum)
    averages = (qkv_average, out_average, gateup_average, down_average, gains_average)
    new_moments = tuple(
        (MOMENTUM * previous + gradient for previous, gradient in zip(moments, totals))
    )
    updated = tuple(
        (
            master - LEARN_RATE * (gradient + MOMENTUM * moment)
            for master, gradient, moment in zip(masters, totals, new_moments)
        )
    )
    averaged = tuple(
        (
            AVERAGE_RATE * previous + (1.0 - AVERAGE_RATE) * weight
            for previous, weight in zip(averages, updated)
        )
    )
    return (
        (jnp.stack(results), jnp.stack(input_grads))
        + tuple(totals)
        + new_moments
        + updated
        + averaged
    )


def solution(mesh):
    return jax.shard_map(
        body,
        mesh=mesh,
        in_specs=(
            P(None, "dp", None),
            P(None, "dp", None),
            P(),
            P("dp", None, "tensor"),
            P("dp", "tensor"),
            P("dp", None, "tensor"),
            P("dp", "tensor"),
            P("dp", None),
            P("dp", None, "tensor"),
            P("dp", "tensor"),
            P("dp", None, "tensor"),
            P("dp", "tensor"),
            P("dp", None),
            P("dp", None, "tensor"),
            P("dp", "tensor"),
            P("dp", None, "tensor"),
            P("dp", "tensor"),
            P("dp", None),
        ),
        out_specs=(
            P(None, "dp", None),
            P(None, "dp", None),
            P("dp", None, "tensor"),
            P("dp", "tensor"),
            P("dp", None, "tensor"),
            P("dp", "tensor"),
            P("dp", None),
            P("dp", None, "tensor"),
            P("dp", "tensor"),
            P("dp", None, "tensor"),
            P("dp", "tensor"),
            P("dp", None),
            P("dp", None, "tensor"),
            P("dp", "tensor"),
            P("dp", None, "tensor"),
            P("dp", "tensor"),
            P("dp", None),
            P("dp", None, "tensor"),
            P("dp", "tensor"),
            P("dp", None, "tensor"),
            P("dp", "tensor"),
            P("dp", None),
        ),
        check_vma=False,
    )
```

profile of v0, /device:TPU:0, one launch (start us, length us, event | category | flops | bytes accessed | tf_op | source)
XLA Modules:
  0.0 908.0 jit_solution(874168385717380845)
XLA Ops:
  7.2 1.7 convert_element_type.219
  9.7 23.1 %all-gather = bf16[16,48,2]{1,2,0:T(2,128)(2,1)S(1)} all-gather(bf16[1,48,2]{1,2,0:T(2,128)(2,1)S(1)} %convert_bitcast_fusion), channel_id=1, replica_groups=mesh['tensor'=2,'dp'=16] {'dp'}, dimensions={0}, use_global_device_ids=true | all-gather | bytes 3264 | tf_op jit(solution)/shard_map/all_gather | solution.py:212
  37.1 21.0 %all_gather.22 = bf16[768,384]{1,0:T(8,128)(2,1)S(1)} all-gather(bf16[48,384]{1,0:T(8,128)(2,1)S(1)} %convert_element_type.228), channel_id=1, replica_groups=mesh['tensor'=2,'dp'=16] {'dp'}, dimensions={0}, use_global_device_ids=true | all-gather | bytes 626688 | tf_op jit(solution)/shard_map/all_gather | solution.py:209
  58.1 2.2 fusion.152
  64.1 2.2 fusion.149
  68.3 1.9 copy.154
  70.2 1.9 copy.153
  74.3 2.4 fusion.91
  76.7 3.1 collective-permute-start.7
  79.8 2.8 collective-permute-start.6
  85.5 2.2 collective-permute-start.4
  88.9 1.9 collective-permute-start.3
  90.9 1.8 collective-permute-start.2
  92.7 2.3 collective-permute-start.1
  95.0 2.3 fusion.161
  98.7 5.4 collective-permute-start
  106.6 2.5 fusion.44
  114.4 49.1 %all-reduce.15.cloned.1.call-done = (f32[256,768]{1,0:T(8,128)}, f32[256,768]{1,0:T(8,128)}) async-done(((f32[256,768]{1,0:T(8,128)}, f32[256,768]{1,0:T(8,128)}), (f32[256,768]{1,0:T(8,128)}, f32[256,768]{1,0:T(8,128)})) %all-reduce.15.cloned.1.call-update) | async-done | bytes 1572880 | tf_op jit(solution)/shard_map/psum | solution.py:101
  165.2 54.3 %all-gather.7.cloned.1.call-done = bf16[768,2,1536]{2,0,1:T(8,128)(2,1)} async-done(((bf16[48,2,1536]{2,0,1:T(8,128)(2,1)}), bf16[768,2,1536]{2,0,1:T(8,128)(2,1)}) %all-gather.7.cloned.1.call-update) | async-done | bytes 4718608 | tf_op jit(solution)/shard_map/all_gather | solution.py:210
  219.6 3.9 fusion.124
  226.6 1.7 copy-done.9
  228.3 3.2 add_bitcast_fusion
  231.5 6.1 copy.189
  237.7 74.3 %reduce-scatter.16.cloned.1.call-done = f32[48,1536]{1,0:T(8,128)} async-done(((f32[768,1536]{1,0:T(8,128)}), f32[48,1536]{1,0:T(8,128)}) %reduce-scatter.16.cloned.1.call-update) | async-done | bytes 294928
  312.0 2.3 multiply_add_fusion.2
  314.5 41.7 %all-gather.9.cloned.1.call-done = bf16[768,1536]{1,0:T(8,128)(2,1)} async-done(((bf16[48,1536]{1,0:T(8,128)(2,1)}), bf16[768,1536]{1,0:T(8,128)(2,1)}) %all-gather.9.cloned.1.call-update) | async-done | bytes 2359312 | tf_op jit(solution)/shard_map/all_gather | solution.py:211
  356.2 3.9 fusion.73
  362.7 2.3 convolution_bitcast_fusion.1
  365.0 2.3 convolution_bitcast_fusion
  367.5 4.5 convolution_convert_fusion
  372.0 1.8 convolution_convert_fusion.1
  373.8 44.0 %all-reduce.13.cloned.1.call-done = (f32[256,768]{1,0:T(8,128)}, f32[256,768]{1,0:T(8,128)}) async-done(((f32[256,768]{1,0:T(8,128)}, f32[256,768]{1,0:T(8,128)}), (f32[256,768]{1,0:T(8,128)}, f32[256,768]{1,0:T(8,128)})) %all-reduce.13.cloned.1.call-update) | async-done | bytes 1572880 | tf_op jit(solution)/shard_map/psum | solution.py:124
  417.8 2.4 multiply_reduce_fusion.3
  420.2 35.5 %all-reduce.17.cloned.1.call-done = (bf16[256,768]{1,0:T(8,128)(2,1)}, bf16[256,768]{1,0:T(8,128)(2,1)}) async-done(((bf16[256,768]{1,0:T(8,128)(2,1)}, bf16[256,768]{1,0:T(8,128)(2,1)}), (bf16[256,768]{1,0:T(8,128)(2,1)}, bf16[256,768]{1,0:T(8,128)(2,1)})) %all-reduce.17.cloned.1.call-update) | async-done | bytes 786448 | tf_op jit(solution)/shard_map/psum | solution.py:111
  455.7 3.2 multiply_add_fusion.1
  463.3 4.5 fusion.166
  471.2 4.3 fusion.163
  478.9 2.4 multiply_reduce_fusion
  485.4 1.8 multiply_reduce_fusion.1
  488.3 1.7 fusion.164
  490.0 2.0 convolution_bitcast_fusion.4
  493.9 1.7 copy.160
  495.7 1.7 copy.164
  497.4 1.8 fusion.156
  501.8 1.9 fusion.86
  503.7 1.7 copy.162
  506.8 1.9 fusion.83
  508.6 1.7 copy.166
  511.8 7.5 collective-permute-done.9
  520.8 2.3 fusion.97
  523.1 1.7 copy.161
  526.7 3.4 convolution_bitcast_fusion.2
  536.7 3.6 fusion.110
  540.3 47.0 %all-reduce.11.cloned.1.call-done = (f32[256,768]{1,0:T(8,128)}, f32[256,768]{1,0:T(8,128)}) async-done(((f32[256,768]{1,0:T(8,128)}, f32[256,768]{1,0:T(8,128)}), (f32[256,768]{1,0:T(8,128)}, f32[256,768]{1,0:T(8,128)})) %all-reduce.11.cloned.1.call-update) | async-done | bytes 1572880 | tf_op jit(solution)/shard_map/psum | solution.py:173
  587.4 2.5 fusion.53
  592.2 4.8 convolution_add_fusion.1
  597.7 3.0 fusion.46
  600.7 5.2 convolution_add_fusion
  607.0 2.0 pad_maximum_fusion.7
  612.6 37.2 %reduce-scatter.12.cloned.1.call-done = f32[48,384]{1,0:T(8,128)} async-done(((f32[768,384]{1,0:T(8,128)}), f32[48,384]{1,0:T(8,128)}) %reduce-scatter.12.cloned.1.call-update) | async-done | bytes 73744 | tf_op jit(solution)/shard_map/reduce_scatter | solution.py:219
  651.4 57.3 %reduce-scatter.18.cloned.1.call-done = f32[48,2]{1,0:T(8,128)} async-done(((f32[768,2]{1,0:T(8,128)}), f32[48,2]{1,0:T(8,128)}) %reduce-scatter.18.cloned.1.call-update) | async-done | bytes 400
  710.1 70.2 %reduce-scatter.10.cloned.1.call-done = f32[48,3,384]{2,0,1:T(8,128)} async-done(((f32[768,3,384]{2,0,1:T(8,128)}), f32[48,3,384]{2,0,1:T(8,128)}) %reduce-scatter.10.cloned.1.call-update) | async-done | bytes 221200 | tf_op jit(solution)/shard_map/reduce_scatter | solution.py:218
  780.4 1.8 multiply_add_fusion.4
  782.2 112.1 %reduce-scatter.14.cloned.1.call-done = f32[48,2,1536]{2,0,1:T(8,128)} async-done(((f32[768,2,1536]{2,0,1:T(8,128)}), f32[48,2,1536]{2,0,1:T(8,128)}) %reduce-scatter.14.cloned.1.call-update) | async-done | bytes 589840 | tf_op jit(solution)/shard_map/reduce_scatter | solution.py:220
  (338 shorter events, 83.8 us)
Async XLA Ops:
  7.2 50.9 %copy-start.2 = (bf16[2,256,768]{2,1,0:T(8,128)(2,1)S(1)}, bf16[2,256,768]{2,1,0:T(8,128)(2,1)}, u32[]{:S(2)}) copy-start(bf16[2,256,768]{2,1,0:T(8,128)(2,1)} %param.18) | copy-start | bytes 2359300
  7.2 50.9 %all-gather.5.cloned.1.call-start = ((), (), s32[]{:S(2)}) async-start(), calls=%async_computation.5 | async-start | bytes 1880064 | tf_op jit(solution)/shard_map/all_gather | solution.py:208
  8.9 154.6 %all-reduce.15.cloned.1.call-start = ((), (), s32[]{:S(2)}) async-start(), calls=%async_computation.15 | async-start | bytes 3145728 | tf_op jit(solution)/shard_map/psum | solution.py:101
  35.6 38.6 %copy-start.51 = (f32[256,64]{0,1:T(8,128)}, f32[256,64]{0,1:T(8,128)S(1)}, u32[]{:S(2)}) copy-start(f32[256,64]{0,1:T(8,128)S(1)} %get-tuple-element.207) | copy-start | bytes 196612
  35.6 38.6 %copy-start.53 = (f32[256,64]{0,1:T(8,128)}, f32[256,64]{0,1:T(8,128)S(1)}, u32[]{:S(2)}) copy-start(f32[256,64]{0,1:T(8,128)S(1)} %get-tuple-element.206) | copy-start | bytes 196612
  37.1 23.3 %copy-start.81 = (f32[256]{0:T(256)}, f32[256]{0:T(256)S(1)}, u32[]{:S(2)}) copy-start(f32[256]{0:T(256)S(1)} %get-tuple-element.231) | copy-start | bytes 3076
  37.1 27.0 %copy-start.79 = (f32[256]{0:T(256)}, f32[256]{0:T(256)S(1)}, u32[]{:S(2)}) copy-start(f32[256]{0:T(256)S(1)} %get-tuple-element.232) | copy-start | bytes 3076
  76.7 12.2 %copy-start.32 = (bf16[256,6,64]{0,2,1:T(8,128)(2,1)S(1)}, bf16[256,6,64]{0,2,1:T(8,128)(2,1)}, u32[]{:S(2)}) copy-start(bf16[256,6,64]{0,2,1:T(8,128)(2,1)} %get-tuple-element.192) | copy-start | bytes 589828
  76.7 18.3 %copy-start.36 = (bf16[256,6,64]{0,2,1:T(8,128)(2,1)S(1)}, bf16[256,6,64]{0,2,1:T(8,128)(2,1)}, u32[]{:S(2)}) copy-start(bf16[256,6,64]{0,2,1:T(8,128)(2,1)} %get-tuple-element.193) | copy-start | bytes 589828
  76.7 14.2 %collective-permute-start.7 = (bf16[256,6,64]{0,2,1:T(8,128)(2,1)}, bf16[256,6,64]{0,2,1:T(8,128)(2,1)}, u32[]{:S(2)}, u32[]{:S(2)}) collective-permute-start(bf16[256,6,64]{0,2,1:T(8,128)(2,1)} %get-tuple-element.194), channel_id=1, source_target_pairs={{0,1},{1,2},{2,3},{3,4},{4,5},{5,6},{6,7},{7,8},{8,9},{9,10},{10,1... | collective-permute-start | bytes 589832 | tf_op jit(solution)/shard_map/ppermute | solution.py:19
  79.8 12.9 %collective-permute-start.6 = (bf16[256,6,64]{0,2,1:T(8,128)(2,1)}, bf16[256,6,64]{0,2,1:T(8,128)(2,1)}, u32[]{:S(2)}, u32[]{:S(2)}) collective-permute-start(bf16[256,6,64]{0,2,1:T(8,128)(2,1)} %get-tuple-element.194), channel_id=1, source_target_pairs={{0,2},{1,3},{2,4},{3,5},{4,6},{5,7},{6,8},{7,9},{8,10},{9,11},{10,... | collective-permute-start | bytes 589832 | tf_op jit(solution)/shard_map/ppermute | solution.py:19
  83.9 22.7 %copy-start.46 = (bf16[256,1,384]{0,2,1:T(8,128)(2,1)}, bf16[256,1,384]{0,2,1:T(8,128)(2,1)S(1)}, u32[]{:S(2)}) copy-start(bf16[256,1,384]{0,2,1:T(8,128)(2,1)S(1)} %copy.156) | copy-start | bytes 589828
  83.9 22.6 %collective-permute-start.5 = (bf16[256,6,64]{0,2,1:T(8,128)(2,1)S(1)}, bf16[256,6,64]{0,2,1:T(8,128)(2,1)S(1)}, u32[]{:S(2)}, u32[]{:S(2)}) collective-permute-start(bf16[256,6,64]{0,2,1:T(8,128)(2,1)S(1)} %bitcast.272), channel_id=1, source_target_pairs={{0,1},{1,2},{2,3},{3,4},{4,5},{5,6},{6,7},{7,8},{8,9},{9,10},{10,1... | collective-permute-start | bytes 589832 | tf_op jit(solution)/shard_map/ppermute | solution.py:19
  85.5 21.0 %collective-permute-start.4 = (bf16[256,6,64]{0,2,1:T(8,128)(2,1)S(1)}, bf16[256,6,64]{0,2,1:T(8,128)(2,1)}, u32[]{:S(2)}, u32[]{:S(2)}) collective-permute-start(bf16[256,6,64]{0,2,1:T(8,128)(2,1)S(1)} %bitcast.273), channel_id=1, source_target_pairs={{0,2},{1,3},{2,4},{3,5},{4,6},{5,7},{6,8},{7,9},{8,10},{9,11},{10,... | collective-permute-start | bytes 589832 | tf_op jit(solution)/shard_map/ppermute | solution.py:19
  88.9 21.5 %copy-start.44 = (bf16[256,1,384]{0,2,1:T(8,128)(2,1)}, bf16[256,1,384]{0,2,1:T(8,128)(2,1)S(1)}, u32[]{:S(2)}) copy-start(bf16[256,1,384]{0,2,1:T(8,128)(2,1)S(1)} %copy.152) | copy-start | bytes 589828
  88.9 9.7 %collective-permute-start.3 = (bf16[256,6,64]{0,2,1:T(8,128)(2,1)S(1)}, bf16[256,6,64]{0,2,1:T(8,128)(2,1)S(1)}, u32[]{:S(2)}, u32[]{:S(2)}) collective-permute-start(bf16[256,6,64]{0,2,1:T(8,128)(2,1)S(1)} %copy-done.32), channel_id=1, source_target_pairs={{0,1},{1,2},{2,3},{3,4},{4,5},{5,6},{6,7},{7,8},{8,9},{9,10},{10,1... | collective-permute-start | bytes 589832 | tf_op jit(solution)/shard_map/ppermute | solution.py:19
  90.9 13.2 %collective-permute-start.2 = (bf16[256,6,64]{0,2,1:T(8,128)(2,1)S(1)}, bf16[256,6,64]{0,2,1:T(8,128)(2,1)S(1)}, u32[]{:S(2)}, u32[]{:S(2)}) collective-permute-start(bf16[256,6,64]{0,2,1:T(8,128)(2,1)S(1)} %copy-done.32), channel_id=1, source_target_pairs={{0,2},{1,3},{2,4},{3,5},{4,6},{5,7},{6,8},{7,9},{8,10},{9,11},{10,... | collective-permute-start | bytes 589832 | tf_op jit(solution)/shard_map/ppermute | solution.py:19
  92.7 17.7 %collective-permute-start.1 = (bf16[256,6,64]{0,2,1:T(8,128)(2,1)S(1)}, bf16[256,6,64]{0,2,1:T(8,128)(2,1)S(1)}, u32[]{:S(2)}, u32[]{:S(2)}) collective-permute-start(bf16[256,6,64]{0,2,1:T(8,128)(2,1)S(1)} %bitcast.268), channel_id=1, source_target_pairs={{0,1},{1,2},{2,3},{3,4},{4,5},{5,6},{6,7},{7,8},{8,9},{9,10},{10,1... | collective-permute-start | bytes 589832 | tf_op jit(solution)/shard_map/ppermute | solution.py:19
  97.3 9.3 %copy-start.1 = (f32[6,256,768]{2,1,0:T(8,128)}, f32[6,256,768]{2,1,0:T(8,128)S(1)}, u32[]{:S(2)}) copy-start(f32[6,256,768]{2,1,0:T(8,128)S(1)} %get-tuple-element.215) | copy-start | bytes 14155780
  97.3 6.8 copy-start.34
  97.3 6.8 copy-start.66
  98.7 6.5 copy-start.62
  98.7 11.7 %collective-permute-start = (bf16[256,6,64]{0,2,1:T(8,128)(2,1)S(1)}, bf16[256,6,64]{0,2,1:T(8,128)(2,1)S(1)}, u32[]{:S(2)}, u32[]{:S(2)}) collective-permute-start(bf16[256,6,64]{0,2,1:T(8,128)(2,1)S(1)} %bitcast.269), channel_id=1, source_target_pairs={{0,2},{1,3},{2,4},{3,5},{4,6},{5,7},{6,8},{7,9},{8,10},{9,11},{10,... | collective-permute-start | bytes 589832 | tf_op jit(solution)/shard_map/ppermute | solution.py:19
  113.4 106.1 %all-gather.7.cloned.1.call-start = ((), (), s32[]{:S(2)}) async-start(), calls=%async_computation.6 | async-start | bytes 5013504 | tf_op jit(solution)/shard_map/all_gather | solution.py:210
  114.3 197.6 %reduce-scatter.16.cloned.1.call-start = ((), (), s32[]{:S(2)}) async-start(), calls=%async_computation.11 | async-start | bytes 5013504
  165.2 290.5 %copy-start.73 = (f32[256]{0:T(256)}, f32[256]{0:T(256)S(1)}, u32[]{:S(2)}) copy-start(f32[256]{0:T(256)S(1)} %add_rsqrt_fusion.2) | copy-start | bytes 3076
  165.2 290.5 %copy-start.77 = (f32[256]{0:T(256)}, f32[256]{0:T(256)S(1)}, u32[]{:S(2)}) copy-start(f32[256]{0:T(256)S(1)} %add_rsqrt_fusion) | copy-start | bytes 3076
  237.6 74.3 %copy-start.56 = (f32[48,1536]{1,0:T(8,128)S(1)}, f32[48,1536]{1,0:T(8,128)}, u32[]{:S(2)}) copy-start(f32[48,1536]{1,0:T(8,128)} %param.34) | copy-start | bytes 884740
  237.7 118.5 %all-gather.9.cloned.1.call-start = ((), (), s32[]{:S(2)}) async-start(), calls=%async_computation.7 | async-start | bytes 2506752 | tf_op jit(solution)/shard_map/all_gather | solution.py:211
  314.3 103.5 %all-reduce.13.cloned.1.call-start = ((), (), s32[]{:S(2)}) async-start(), calls=%async_computation.14 | async-start | bytes 3145728 | tf_op jit(solution)/shard_map/psum | solution.py:124
  367.4 88.3 %all-reduce.17.cloned.1.call-start = ((), (), s32[]{:S(2)}) async-start(), calls=%async_computation.16 | async-start | bytes 1572864 | tf_op jit(solution)/shard_map/psum | solution.py:111
  373.8 213.6 %all-reduce.11.cloned.1.call-start = ((), (), s32[]{:S(2)}) async-start(), calls=%async_computation.13 | async-start | bytes 3145728 | tf_op jit(solution)/shard_map/psum | solution.py:173
  460.1 18.8 %slice-start.2 = ((s8[4718592]{0:T(1024)(128)(4,1)}), s8[524288]{0:T(1024)(128)(4,1)S(1)}, s32[]{:S(2)}) async-start(s8[4718592]{0:T(1024)(128)(4,1)} %bitcast.244), calls=%async_computation.19 | async-start | bytes 1048576
  463.3 15.6 %slice-start.3 = ((s8[4718592]{0:T(1024)(128)(4,1)}), s8[4194304]{0:T(1024)(128)(4,1)S(1)}, s32[]{:S(2)}) async-start(s8[4718592]{0:T(1024)(128)(4,1)} %bitcast.244), calls=%async_computation.20 | async-start | bytes 8388608
  468.6 30.6 %collective-permute-start.10 = (bf16[256,6,64]{0,2,1:T(8,128)(2,1)}, bf16[256,6,64]{0,2,1:T(8,128)(2,1)}, u32[]{:S(2)}, u32[]{:S(2)}) collective-permute-start(bf16[256,6,64]{0,2,1:T(8,128)(2,1)} %get-tuple-element.169), channel_id=1, source_target_pairs={{1,0},{2,1},{3,2},{4,3},{5,4},{6,5},{7,6},{8,7},{9,8},{10,9},{11,1... | collective-permute-start | bytes 589832 | tf_op jit(solution)/shard_map/ppermute | solution.py:19
  469.9 30.7 %collective-permute-start.11 = (bf16[256,6,64]{0,2,1:T(8,128)(2,1)}, bf16[256,6,64]{0,2,1:T(8,128)(2,1)}, u32[]{:S(2)}, u32[]{:S(2)}) collective-permute-start(bf16[256,6,64]{0,2,1:T(8,128)(2,1)} %get-tuple-element.170), channel_id=1, source_target_pairs={{2,0},{3,1},{4,2},{5,3},{6,4},{7,5},{8,6},{9,7},{10,8},{11,9},{12,... | collective-permute-start | bytes 589832 | tf_op jit(solution)/shard_map/ppermute | solution.py:19
  471.2 7.7 copy-start.47
  471.2 7.7 copy-start.68
  476.3 29.2 %collective-permute-start.14 = (bf16[256,6,64]{0,2,1:T(8,128)(2,1)}, bf16[256,6,64]{0,2,1:T(8,128)(2,1)}, u32[]{:S(2)}, u32[]{:S(2)}) collective-permute-start(bf16[256,6,64]{0,2,1:T(8,128)(2,1)} %get-tuple-element.173), channel_id=1, source_target_pairs={{1,0},{2,1},{3,2},{4,3},{5,4},{6,5},{7,6},{8,7},{9,8},{10,9},{11,1... | collective-permute-start | bytes 589832 | tf_op jit(solution)/shard_map/ppermute | solution.py:19
  477.6 29.2 %collective-permute-start.15 = (bf16[256,6,64]{0,2,1:T(8,128)(2,1)}, bf16[256,6,64]{0,2,1:T(8,128)(2,1)}, u32[]{:S(2)}, u32[]{:S(2)}) collective-permute-start(bf16[256,6,64]{0,2,1:T(8,128)(2,1)} %get-tuple-element.174), channel_id=1, source_target_pairs={{2,0},{3,1},{4,2},{5,3},{6,4},{7,5},{8,6},{9,7},{10,8},{11,9},{12,... | collective-permute-start | bytes 589832 | tf_op jit(solution)/shard_map/ppermute | solution.py:19
  483.9 26.5 %collective-permute-start.12 = (bf16[256,6,64]{0,2,1:T(8,128)(2,1)}, bf16[256,6,64]{0,2,1:T(8,128)(2,1)}, u32[]{:S(2)}, u32[]{:S(2)}) collective-permute-start(bf16[256,6,64]{0,2,1:T(8,128)(2,1)} %get-tuple-element.171), channel_id=1, source_target_pairs={{1,0},{2,1},{3,2},{4,3},{5,4},{6,5},{7,6},{8,7},{9,8},{10,9},{11,1... | collective-permute-start | bytes 589832 | tf_op jit(solution)/shard_map/ppermute | solution.py:19
  499.2 12.5 %collective-permute-start.13 = (bf16[256,6,64]{0,2,1:T(8,128)(2,1)}, bf16[256,6,64]{0,2,1:T(8,128)(2,1)}, u32[]{:S(2)}, u32[]{:S(2)}) collective-permute-start(bf16[256,6,64]{0,2,1:T(8,128)(2,1)} %get-tuple-element.172), channel_id=1, source_target_pairs={{2,0},{3,1},{4,2},{5,3},{6,4},{7,5},{8,6},{9,7},{10,8},{11,9},{12,... | collective-permute-start | bytes 589832 | tf_op jit(solution)/shard_map/ppermute | solution.py:19
  500.5 11.2 %collective-permute-start.8 = (bf16[256,6,64]{0,2,1:T(8,128)(2,1)}, bf16[256,6,64]{0,2,1:T(8,128)(2,1)}, u32[]{:S(2)}, u32[]{:S(2)}) collective-permute-start(bf16[256,6,64]{0,2,1:T(8,128)(2,1)} %get-tuple-element.167), channel_id=1, source_target_pairs={{1,0},{2,1},{3,2},{4,3},{5,4},{6,5},{7,6},{8,7},{9,8},{10,9},{11,1... | collective-permute-start | bytes 589832 | tf_op jit(solution)/shard_map/ppermute | solution.py:19
  505.5 13.8 %collective-permute-start.9 = (bf16[256,6,64]{0,2,1:T(8,128)(2,1)}, bf16[256,6,64]{0,2,1:T(8,128)(2,1)}, u32[]{:S(2)}, u32[]{:S(2)}) collective-permute-start(bf16[256,6,64]{0,2,1:T(8,128)(2,1)} %get-tuple-element.168), channel_id=1, source_target_pairs={{2,0},{3,1},{4,2},{5,3},{6,4},{7,5},{8,6},{9,7},{10,8},{11,9},{12,... | collective-permute-start | bytes 589832 | tf_op jit(solution)/shard_map/ppermute | solution.py:19
  531.8 118.0 %reduce-scatter.12.cloned.1.call-start = ((), (), s32[]{:S(2)}) async-start(), calls=%async_computation.9 | async-start | bytes 1253376 | tf_op jit(solution)/shard_map/reduce_scatter | solution.py:219
  534.8 173.9 %reduce-scatter.18.cloned.1.call-start = ((), (), s32[]{:S(2)}) async-start(), calls=%async_computation.12 | async-start | bytes 417792
  536.7 50.6 %copy-start.82 = (f32[256]{0:T(256)S(1)}, f32[256]{0:T(256)}, u32[]{:S(2)}) copy-start(f32[256]{0:T(256)} %copy-done.81) | copy-start | bytes 3076
  540.3 51.9 %copy-start.48 = (bf16[256,1,384]{2,0,1:T(8,128)(2,1)S(1)}, bf16[256,1,384]{2,0,1:T(8,128)(2,1)}, u32[]{:S(2)}) copy-start(bf16[256,1,384]{2,0,1:T(8,128)(2,1)} %copy.164) | copy-start | bytes 589828
  540.3 51.9 %copy-start.49 = (bf16[256,1,384]{2,0,1:T(8,128)(2,1)S(1)}, bf16[256,1,384]{2,0,1:T(8,128)(2,1)}, u32[]{:S(2)}) copy-start(bf16[256,1,384]{2,0,1:T(8,128)(2,1)} %copy.166) | copy-start | bytes 589828
  592.1 188.2 %reduce-scatter.10.cloned.1.call-start = ((), (), s32[]{:S(2)}) async-start(), calls=%async_computation.8 | async-start | bytes 3760128 | tf_op jit(solution)/shard_map/reduce_scatter | solution.py:218
  597.0 297.3 %reduce-scatter.14.cloned.1.call-start = ((), (), s32[]{:S(2)}) async-start(), calls=%async_computation.10 | async-start | bytes 10027008 | tf_op jit(solution)/shard_map/reduce_scatter | solution.py:220
  611.2 38.6 %copy-start.57 = (f32[48,384]{1,0:T(8,128)S(1)}, f32[48,384]{1,0:T(8,128)}, u32[]{:S(2)}) copy-start(f32[48,384]{1,0:T(8,128)} %param.22) | copy-start | bytes 221188
  611.2 38.6 %copy-start.75 = (f32[48,384]{1,0:T(8,128)S(1)}, f32[48,384]{1,0:T(8,128)}, u32[]{:S(2)}) copy-start(f32[48,384]{1,0:T(8,128)} %param.32) | copy-start | bytes 221188
  611.2 38.6 %copy-start.76 = (f32[48,384]{1,0:T(8,128)S(1)}, f32[48,384]{1,0:T(8,128)}, u32[]{:S(2)}) copy-start(f32[48,384]{1,0:T(8,128)} %param.27) | copy-start | bytes 221188
  611.2 98.3 %copy-start.88 = (f32[48,2]{0,1:T(2,128)S(1)}, f32[48,2]{0,1:T(2,128)}, u32[]{:S(2)}) copy-start(f32[48,2]{0,1:T(2,128)} %param.25) | copy-start | bytes 1156
  611.2 98.3 %copy-start.89 = (f32[48,2]{0,1:T(2,128)S(1)}, f32[48,2]{0,1:T(2,128)}, u32[]{:S(2)}) copy-start(f32[48,2]{0,1:T(2,128)} %param.35) | copy-start | bytes 1156
  611.3 98.2 %copy-start.90 = (f32[48,2]{0,1:T(2,128)S(1)}, f32[48,2]{0,1:T(2,128)}, u32[]{:S(2)}) copy-start(f32[48,2]{0,1:T(2,128)} %param.30) | copy-start | bytes 1156
  611.3 169.1 %copy-start.25 = (f32[48,3,384]{2,0,1:T(8,128)S(1)}, f32[48,3,384]{2,0,1:T(8,128)}, u32[]{:S(2)}) copy-start(f32[48,3,384]{2,0,1:T(8,128)} %param.21) | copy-start | bytes 663556
  611.3 169.1 %copy-start.60 = (f32[48,3,384]{2,0,1:T(8,128)S(1)}, f32[48,3,384]{2,0,1:T(8,128)}, u32[]{:S(2)}) copy-start(f32[48,3,384]{2,0,1:T(8,128)} %param.31) | copy-start | bytes 663556
  611.3 169.1 %copy-start.61 = (f32[48,3,384]{2,0,1:T(8,128)S(1)}, f32[48,3,384]{2,0,1:T(8,128)}, u32[]{:S(2)}) copy-start(f32[48,3,384]{2,0,1:T(8,128)} %param.26) | copy-start | bytes 663556
  612.6 281.7 %copy-start.18 = (f32[48,2,1536]{2,1,0:T(2,128)S(1)}, f32[48,2,1536]{2,1,0:T(2,128)}, u32[]{:S(2)}) copy-start(f32[48,2,1536]{2,1,0:T(2,128)} %param.23) | copy-start | bytes 1769476
  612.6 281.7 %copy-start.54 = (f32[48,2,1536]{2,1,0:T(2,128)S(1)}, f32[48,2,1536]{2,1,0:T(2,128)}, u32[]{:S(2)}) copy-start(f32[48,2,1536]{2,1,0:T(2,128)} %param.33) | copy-start | bytes 1769476
  612.6 281.7 %copy-start.55 = (f32[48,2,1536]{2,1,0:T(2,128)S(1)}, f32[48,2,1536]{2,1,0:T(2,128)}, u32[]{:S(2)}) copy-start(f32[48,2,1536]{2,1,0:T(2,128)} %param.28) | copy-start | bytes 1769476
  709.5 186.3 %copy-start.87 = (f32[48,2]{0,1:T(2,128)}, f32[48,2]{0,1:T(2,128)S(1)}, u32[]{:S(2)}) copy-start(f32[48,2]{0,1:T(2,128)S(1)} %copy.192) | copy-start | bytes 1156
  (65 other events, 177.0 us)
Sparse Core Ops, SparseCore 0:
  10.9 45.0 all-gather.4
  113.6 49.9 all-reduce.14
  166.4 53.1 all-gather.6
  237.8 74.1 reduce-scatter.15
  314.7 41.4 all-gather.8
  367.5 50.2 all-reduce.12
  421.3 34.3 all-reduce.16
  531.9 55.4 all-reduce.10
  591.5 58.1 reduce-scatter.11
  653.7 54.9 reduce-scatter.17
  713.1 67.1 reduce-scatter.9
  784.3 109.9 reduce-scatter.13
where the time goes:
time: 916 us; the launch traced here: 908 us
  waiting for transfers between devices  632 us (69%)
  matrix products  85 us (9%)
  other arithmetic  49.9 us (5%)
  local copies, waits for them, and re-layouts  48.6 us (5%)
  blocking collectives  44.1 us (5%)
  starting transfers between devices  32.5 us (4%)
  between operations  16 us (2%)
    unnamed x14, waiting for transfers between devices  132 us
    reduce_scatter x1, waiting for transfers between devices, body(): lax.psum_scatter(local_grads[2], 'dp', scatter_dimension=0, tiled=True)  112 us
    reduce_scatter x1, waiting for transfers between devices, body(): lax.psum_scatter(local_grads[0], 'dp', scatter_dimension=0, tiled=True)  70.2 us
    all_gather x1, waiting for transfers between devices, body(): lax.all_gather(shards[2], 'dp', axis=0, tiled=True)  54.3 us
    psum x1, waiting for transfers between devices, micro_step(): branch = lax.psum(branch, 'tensor')  49.1 us
    psum x1, waiting for transfers between devices, micro_step(): grad_normed_one = lax.psum(grad_normed_one, 'tensor')  47 us
    psum x1, waiting for transfers between devices, micro_step(): grad_normed_two = lax.psum(grad_normed_two, 'tensor')  44 us
    all_gather x1, waiting for transfers between devices, body(): lax.all_gather(shards[3], 'dp', axis=0, tiled=True)  41.7 us
  transfers between devices with their start and end apart: 28, of which 13 were waited for; matrix products, arithmetic and copies ran while one was open for 11% of the time, Pallas kernels for 0%

commit v1 on v0

--- a/solution.py
+++ b/solution.py
@@ -108,7 +108,9 @@
     active = gate * sigma
     hidden = (active * upward).astype(jnp.bfloat16)
     down_part = jnp.einsum("tf,df->td", hidden, down_full, preferred_element_type=jnp.float32)
-    down_part = lax.psum(down_part.astype(jnp.bfloat16), "tensor").astype(jnp.float32)
+    down_part = jnp.sum(lax.all_gather(down_part.astype(jnp.bfloat16), "tensor"), axis=0).astype(
+        jnp.float32
+    )
     result = (resid + down_part).astype(jnp.bfloat16)
     grad_hidden = jnp.einsum("td,df->tf", upstream, down_full, preferred_element_type=jnp.float32)
     down_grad = jnp.einsum("td,tf->df", upstream, hidden, preferred_element_type=jnp.float32)

time: 916 us -> 887 us (0.968)
  waiting for transfers between devices: 632 us -> 569 us
  blocking collectives: 44.1 us -> 76.2 us
    psum x1 -> x0, waiting for transfers between devices: 35.5 us -> none  [micro_step(): lax.psum(down_part.astype(jnp.bfloat16), 'tensor').astype(jnp.float32)]
    all_gather x0 -> x2, blocking collectives: none -> 32 us  [micro_step(): lax.all_gather(down_part.astype(jnp.bfloat16), 'tensor')]
    psum x1, waiting for transfers between devices: 44 us -> 16.3 us  [micro_step(): grad_normed_two = lax.psum(grad_normed_two, 'tensor')]
    unnamed x14 -> x13, waiting for transfers between devices: 132 us -> 132 us
    unnamed x211 -> x215, local copies, waits for them, and re-layouts: 21.6 us -> 21.7 us
  transfers between devices with their start and end apart: 28 -> 27, of which waited for: 13 -> 12; matrix products, arithmetic and copies ran while one was open for 11% -> 11% of each run, Pallas kernels for 0% -> 0%
where the time goes in v1:
time: 887 us; the launch traced here: 880 us
  waiting for transfers between devices  569 us (64%)
  matrix products  85.9 us (10%)
  blocking collectives  76.2 us (9%)
  other arithmetic  51.7 us (6%)
  local copies, waits for them, and re-layouts  48.7 us (5%)
  starting transfers between devices  32.5 us (4%)
  between operations  15.7 us (2%)
    unnamed x13, waiting for transfers between devices  132 us
    reduce_scatter x1, waiting for transfers between devices, body(): lax.psum_scatter(local_grads[2], 'dp', scatter_dimension=0, tiled=True)  112 us
    reduce_scatter x1, waiting for transfers between devices, body(): lax.psum_scatter(local_grads[0], 'dp', scatter_dimension=0, tiled=True)  70 us
    all_gather x1, waiting for transfers between devices, body(): lax.all_gather(shards[2], 'dp', axis=0, tiled=True)  54.3 us
    psum x1, waiting for transfers between devices, micro_step(): branch = lax.psum(branch, 'tensor')  49.2 us
    psum x1, waiting for transfers between devices, micro_step(): grad_normed_one = lax.psum(grad_normed_one, 'tensor')  47 us
    all_gather x1, waiting for transfers between devices, body(): lax.all_gather(shards[3], 'dp', axis=0, tiled=True)  41.7 us
    reduce_scatter x1, waiting for transfers between devices, body(): lax.psum_scatter(local_grads[1], 'dp', scatter_dimension=0, tiled=True)  37.2 us
  transfers between devices with their start and end apart: 27, of which 12 were waited for; matrix products, arithmetic and copies ran while one was open for 11% of the time, Pallas kernels for 0%

profile of v1, /device:TPU:0, one launch (start us, length us, event | category | flops | bytes accessed | tf_op | source)
XLA Modules:
  0.0 879.7 jit_solution(1725547502948946318)
XLA Ops:
  9.7 23.1 %all-gather.2 = bf16[16,48,2]{1,2,0:T(2,128)(2,1)S(1)} all-gather(bf16[1,48,2]{1,2,0:T(2,128)(2,1)S(1)} %convert_bitcast_fusion), channel_id=1, replica_groups=mesh['tensor'=2,'dp'=16] {'dp'}, dimensions={0}, use_global_device_ids=true | all-gather | bytes 3264 | tf_op jit(solution)/shard_map/all_gather | solution.py:214
  37.1 21.0 %all_gather.34 = bf16[768,384]{1,0:T(8,128)(2,1)S(1)} all-gather(bf16[48,384]{1,0:T(8,128)(2,1)S(1)} %convert_element_type.232), channel_id=1, replica_groups=mesh['tensor'=2,'dp'=16] {'dp'}, dimensions={0}, use_global_device_ids=true | all-gather | bytes 626688 | tf_op jit(solution)/shard_map/all_gather | solution.py:211
  58.1 2.2 fusion.152
  64.1 2.2 fusion.149
  68.3 1.9 copy.154
  70.2 1.9 copy.153
  74.3 2.4 fusion.91
  76.7 3.1 collective-permute-start.7
  79.8 2.8 collective-permute-start.6
  85.5 2.2 collective-permute-start.4
  89.0 1.9 collective-permute-start.3
  90.9 1.8 collective-permute-start.2
  92.7 2.3 collective-permute-start.1
  95.0 2.3 fusion.161
  98.7 5.4 collective-permute-start
  106.6 2.5 fusion.44
  114.4 49.2 %all-reduce.13.cloned.1.call-done = (f32[256,768]{1,0:T(8,128)}, f32[256,768]{1,0:T(8,128)}) async-done(((f32[256,768]{1,0:T(8,128)}, f32[256,768]{1,0:T(8,128)}), (f32[256,768]{1,0:T(8,128)}, f32[256,768]{1,0:T(8,128)})) %all-reduce.13.cloned.1.call-update) | async-done | bytes 1572880 | tf_op jit(solution)/shard_map/psum | solution.py:101
  165.2 54.3 %all-gather.9.cloned.1.call-done = bf16[768,2,1536]{2,0,1:T(8,128)(2,1)} async-done(((bf16[48,2,1536]{2,0,1:T(8,128)(2,1)}), bf16[768,2,1536]{2,0,1:T(8,128)(2,1)}) %all-gather.9.cloned.1.call-update) | async-done | bytes 4718608 | tf_op jit(solution)/shard_map/all_gather | solution.py:212
  219.6 3.9 fusion.124
  226.6 1.7 copy-done.9
  228.3 3.3 add_bitcast_fusion
  231.6 6.1 copy.189
  237.8 74.3 %reduce-scatter.16.cloned.1.call-done = f32[48,1536]{1,0:T(8,128)} async-done(((f32[768,1536]{1,0:T(8,128)}), f32[48,1536]{1,0:T(8,128)}) %reduce-scatter.16.cloned.1.call-update) | async-done | bytes 294928
  312.1 2.3 multiply_add_fusion.2
  314.6 41.7 %all-gather.11.cloned.1.call-done = bf16[768,1536]{1,0:T(8,128)(2,1)} async-done(((bf16[48,1536]{1,0:T(8,128)(2,1)}), bf16[768,1536]{1,0:T(8,128)(2,1)}) %all-gather.11.cloned.1.call-update) | async-done | bytes 2359312 | tf_op jit(solution)/shard_map/all_gather | solution.py:213
  356.3 3.9 fusion.73
  362.8 2.3 convolution_bitcast_fusion.1
  365.1 2.3 convolution_bitcast_fusion
  367.5 3.6 convolution_convert_fusion
  371.2 20.9 %all-gather.1 = bf16[512,768]{1,0:T(8,128)(2,1)} all-gather(bf16[256,768]{1,0:T(8,128)(2,1)S(1)} %convolution_convert_fusion), channel_id=3, replica_groups=mesh['tensor'=2,'dp'=16] {'tensor'}, dimensions={0}, use_global_device_ids=true | all-gather | bytes 1179648 | tf_op jit(solution)/shard_map/all_gather | solution.py:111
  393.3 3.6 convolution_convert_fusion.1
  397.0 11.2 %all-gather = bf16[512,768]{1,0:T(8,128)(2,1)} all-gather(bf16[256,768]{1,0:T(8,128)(2,1)S(1)} %convolution_convert_fusion.1), channel_id=2, replica_groups=mesh['tensor'=2,'dp'=16] {'tensor'}, dimensions={0}, use_global_device_ids=true | all-gather | bytes 1179648 | tf_op jit(solution)/shard_map/all_gather | solution.py:111
  408.1 2.2 reduce_sum.171
  410.3 16.3 %all-reduce.11.cloned.1.call-done = (f32[256,768]{1,0:T(8,128)}, f32[256,768]{1,0:T(8,128)}) async-done(((f32[256,768]{1,0:T(8,128)}, f32[256,768]{1,0:T(8,128)}), (f32[256,768]{1,0:T(8,128)}, f32[256,768]{1,0:T(8,128)})) %all-reduce.11.cloned.1.call-update) | async-done | bytes 1572880 | tf_op jit(solution)/shard_map/psum | solution.py:126
  426.6 2.6 multiply_reduce_fusion.3
  435.1 4.4 fusion.166
  442.9 4.3 fusion.163
  450.9 2.4 multiply_reduce_fusion
  457.2 1.8 multiply_reduce_fusion.1
  460.0 1.7 fusion.164
  461.8 2.0 convolution_bitcast_fusion.4
  465.7 1.7 copy.160
  467.4 1.7 copy.164
  469.2 1.8 fusion.156
  473.6 1.9 fusion.86
  475.4 1.7 copy.162
  478.5 1.9 fusion.83
  480.4 1.7 copy.166
  483.5 7.5 collective-permute-done.9
  492.5 2.3 fusion.97
  494.9 1.7 copy.161
  498.4 3.4 convolution_bitcast_fusion.2
  508.4 3.6 fusion.110
  512.0 47.0 %all-reduce.9.cloned.1.call-done = (f32[256,768]{1,0:T(8,128)}, f32[256,768]{1,0:T(8,128)}) async-done(((f32[256,768]{1,0:T(8,128)}, f32[256,768]{1,0:T(8,128)}), (f32[256,768]{1,0:T(8,128)}, f32[256,768]{1,0:T(8,128)})) %all-reduce.9.cloned.1.call-update) | async-done | bytes 1572880 | tf_op jit(solution)/shard_map/psum | solution.py:175
  559.1 2.5 fusion.53
  563.9 4.8 convolution_add_fusion.1
  569.4 3.0 fusion.46
  572.4 5.2 convolution_add_fusion
  578.7 2.0 pad_maximum_fusion.7
  584.3 37.2 %reduce-scatter.12.cloned.1.call-done = f32[48,384]{1,0:T(8,128)} async-done(((f32[768,384]{1,0:T(8,128)}), f32[48,384]{1,0:T(8,128)}) %reduce-scatter.12.cloned.1.call-update) | async-done | bytes 73744 | tf_op jit(solution)/shard_map/reduce_scatter | solution.py:221
  623.1 57.6 %reduce-scatter.18.cloned.1.call-done = f32[48,2]{1,0:T(8,128)} async-done(((f32[768,2]{1,0:T(8,128)}), f32[48,2]{1,0:T(8,128)}) %reduce-scatter.18.cloned.1.call-update) | async-done | bytes 400
  682.0 70.0 %reduce-scatter.10.cloned.1.call-done = f32[48,3,384]{2,0,1:T(8,128)} async-done(((f32[768,3,384]{2,0,1:T(8,128)}), f32[48,3,384]{2,0,1:T(8,128)}) %reduce-scatter.10.cloned.1.call-update) | async-done | bytes 221200 | tf_op jit(solution)/shard_map/reduce_scatter | solution.py:220
  752.1 1.8 multiply_add_fusion.4
  753.9 112.3 %reduce-scatter.14.cloned.1.call-done = f32[48,2,1536]{2,0,1:T(8,128)} async-done(((f32[768,2,1536]{2,0,1:T(8,128)}), f32[48,2,1536]{2,0,1:T(8,128)}) %reduce-scatter.14.cloned.1.call-update) | async-done | bytes 589840 | tf_op jit(solution)/shard_map/reduce_scatter | solution.py:222
  (343 shorter events, 88.1 us)
Async XLA Ops:
  7.2 50.9 %copy-start.2 = (bf16[2,256,768]{2,1,0:T(8,128)(2,1)S(1)}, bf16[2,256,768]{2,1,0:T(8,128)(2,1)}, u32[]{:S(2)}) copy-start(bf16[2,256,768]{2,1,0:T(8,128)(2,1)} %param.18) | copy-start | bytes 2359300
  7.2 50.9 %all-gather.7.cloned.1.call-start = ((), (), s32[]{:S(2)}) async-start(), calls=%async_computation.5 | async-start | bytes 1880064 | tf_op jit(solution)/shard_map/all_gather | solution.py:210
  8.9 154.6 %all-reduce.13.cloned.1.call-start = ((), (), s32[]{:S(2)}) async-start(), calls=%async_computation.15 | async-start | bytes 3145728 | tf_op jit(solution)/shard_map/psum | solution.py:101
  35.6 38.6 %copy-start.54 = (f32[256,64]{0,1:T(8,128)}, f32[256,64]{0,1:T(8,128)S(1)}, u32[]{:S(2)}) copy-start(f32[256,64]{0,1:T(8,128)S(1)} %get-tuple-element.205) | copy-start | bytes 196612
  35.6 38.6 %copy-start.56 = (f32[256,64]{0,1:T(8,128)}, f32[256,64]{0,1:T(8,128)S(1)}, u32[]{:S(2)}) copy-start(f32[256,64]{0,1:T(8,128)S(1)} %get-tuple-element.204) | copy-start | bytes 196612
  37.1 23.3 %copy-start.84 = (f32[256]{0:T(256)}, f32[256]{0:T(256)S(1)}, u32[]{:S(2)}) copy-start(f32[256]{0:T(256)S(1)} %get-tuple-element.229) | copy-start | bytes 3076
  37.1 27.0 %copy-start.82 = (f32[256]{0:T(256)}, f32[256]{0:T(256)S(1)}, u32[]{:S(2)}) copy-start(f32[256]{0:T(256)S(1)} %get-tuple-element.230) | copy-start | bytes 3076
  76.7 12.3 %copy-start.35 = (bf16[256,6,64]{0,2,1:T(8,128)(2,1)S(1)}, bf16[256,6,64]{0,2,1:T(8,128)(2,1)}, u32[]{:S(2)}) copy-start(bf16[256,6,64]{0,2,1:T(8,128)(2,1)} %get-tuple-element.190) | copy-start | bytes 589828
  76.7 18.3 %copy-start.39 = (bf16[256,6,64]{0,2,1:T(8,128)(2,1)S(1)}, bf16[256,6,64]{0,2,1:T(8,128)(2,1)}, u32[]{:S(2)}) copy-start(bf16[256,6,64]{0,2,1:T(8,128)(2,1)} %get-tuple-element.191) | copy-start | bytes 589828
  76.7 14.2 %collective-permute-start.7 = (bf16[256,6,64]{0,2,1:T(8,128)(2,1)}, bf16[256,6,64]{0,2,1:T(8,128)(2,1)}, u32[]{:S(2)}, u32[]{:S(2)}) collective-permute-start(bf16[256,6,64]{0,2,1:T(8,128)(2,1)} %get-tuple-element.192), channel_id=1, source_target_pairs={{0,1},{1,2},{2,3},{3,4},{4,5},{5,6},{6,7},{7,8},{8,9},{9,10},{10,1... | collective-permute-start | bytes 589832 | tf_op jit(solution)/shard_map/ppermute | solution.py:19
  79.8 12.9 %collective-permute-start.6 = (bf16[256,6,64]{0,2,1:T(8,128)(2,1)}, bf16[256,6,64]{0,2,1:T(8,128)(2,1)}, u32[]{:S(2)}, u32[]{:S(2)}) collective-permute-start(bf16[256,6,64]{0,2,1:T(8,128)(2,1)} %get-tuple-element.192), channel_id=1, source_target_pairs={{0,2},{1,3},{2,4},{3,5},{4,6},{5,7},{6,8},{7,9},{8,10},{9,11},{10,... | collective-permute-start | bytes 589832 | tf_op jit(solution)/shard_map/ppermute | solution.py:19
  83.9 22.7 %copy-start.49 = (bf16[256,1,384]{0,2,1:T(8,128)(2,1)}, bf16[256,1,384]{0,2,1:T(8,128)(2,1)S(1)}, u32[]{:S(2)}) copy-start(bf16[256,1,384]{0,2,1:T(8,128)(2,1)S(1)} %copy.156) | copy-start | bytes 589828
  83.9 22.6 %collective-permute-start.5 = (bf16[256,6,64]{0,2,1:T(8,128)(2,1)S(1)}, bf16[256,6,64]{0,2,1:T(8,128)(2,1)S(1)}, u32[]{:S(2)}, u32[]{:S(2)}) collective-permute-start(bf16[256,6,64]{0,2,1:T(8,128)(2,1)S(1)} %bitcast.276), channel_id=1, source_target_pairs={{0,1},{1,2},{2,3},{3,4},{4,5},{5,6},{6,7},{7,8},{8,9},{9,10},{10,1... | collective-permute-start | bytes 589832 | tf_op jit(solution)/shard_map/ppermute | solution.py:19
  85.5 21.0 %collective-permute-start.4 = (bf16[256,6,64]{0,2,1:T(8,128)(2,1)S(1)}, bf16[256,6,64]{0,2,1:T(8,128)(2,1)}, u32[]{:S(2)}, u32[]{:S(2)}) collective-permute-start(bf16[256,6,64]{0,2,1:T(8,128)(2,1)S(1)} %bitcast.277), channel_id=1, source_target_pairs={{0,2},{1,3},{2,4},{3,5},{4,6},{5,7},{6,8},{7,9},{8,10},{9,11},{10,... | collective-permute-start | bytes 589832 | tf_op jit(solution)/shard_map/ppermute | solution.py:19
  88.9 21.5 %copy-start.47 = (bf16[256,1,384]{0,2,1:T(8,128)(2,1)}, bf16[256,1,384]{0,2,1:T(8,128)(2,1)S(1)}, u32[]{:S(2)}) copy-start(bf16[256,1,384]{0,2,1:T(8,128)(2,1)S(1)} %copy.152) | copy-start | bytes 589828
  89.0 9.7 %collective-permute-start.3 = (bf16[256,6,64]{0,2,1:T(8,128)(2,1)S(1)}, bf16[256,6,64]{0,2,1:T(8,128)(2,1)S(1)}, u32[]{:S(2)}, u32[]{:S(2)}) collective-permute-start(bf16[256,6,64]{0,2,1:T(8,128)(2,1)S(1)} %copy-done.35), channel_id=1, source_target_pairs={{0,1},{1,2},{2,3},{3,4},{4,5},{5,6},{6,7},{7,8},{8,9},{9,10},{10,1... | collective-permute-start | bytes 589832 | tf_op jit(solution)/shard_map/ppermute | solution.py:19
  90.9 13.1 %collective-permute-start.2 = (bf16[256,6,64]{0,2,1:T(8,128)(2,1)S(1)}, bf16[256,6,64]{0,2,1:T(8,128)(2,1)S(1)}, u32[]{:S(2)}, u32[]{:S(2)}) collective-permute-start(bf16[256,6,64]{0,2,1:T(8,128)(2,1)S(1)} %copy-done.35), channel_id=1, source_target_pairs={{0,2},{1,3},{2,4},{3,5},{4,6},{5,7},{6,8},{7,9},{8,10},{9,11},{10,... | collective-permute-start | bytes 589832 | tf_op jit(solution)/shard_map/ppermute | solution.py:19
  92.7 17.7 %collective-permute-start.1 = (bf16[256,6,64]{0,2,1:T(8,128)(2,1)S(1)}, bf16[256,6,64]{0,2,1:T(8,128)(2,1)S(1)}, u32[]{:S(2)}, u32[]{:S(2)}) collective-permute-start(bf16[256,6,64]{0,2,1:T(8,128)(2,1)S(1)} %bitcast.272), channel_id=1, source_target_pairs={{0,1},{1,2},{2,3},{3,4},{4,5},{5,6},{6,7},{7,8},{8,9},{9,10},{10,1... | collective-permute-start | bytes 589832 | tf_op jit(solution)/shard_map/ppermute | solution.py:19
  97.3 9.3 %copy-start.1 = (f32[6,256,768]{2,1,0:T(8,128)}, f32[6,256,768]{2,1,0:T(8,128)S(1)}, u32[]{:S(2)}) copy-start(f32[6,256,768]{2,1,0:T(8,128)S(1)} %get-tuple-element.213) | copy-start | bytes 14155780
  97.3 6.8 copy-start.37
  97.3 6.8 copy-start.69
  98.7 6.5 copy-start.65
  98.7 11.7 %collective-permute-start = (bf16[256,6,64]{0,2,1:T(8,128)(2,1)S(1)}, bf16[256,6,64]{0,2,1:T(8,128)(2,1)S(1)}, u32[]{:S(2)}, u32[]{:S(2)}) collective-permute-start(bf16[256,6,64]{0,2,1:T(8,128)(2,1)S(1)} %bitcast.273), channel_id=1, source_target_pairs={{0,2},{1,3},{2,4},{3,5},{4,6},{5,7},{6,8},{7,9},{8,10},{9,11},{10,... | collective-permute-start | bytes 589832 | tf_op jit(solution)/shard_map/ppermute | solution.py:19
  113.4 106.1 %all-gather.9.cloned.1.call-start = ((), (), s32[]{:S(2)}) async-start(), calls=%async_computation.6 | async-start | bytes 5013504 | tf_op jit(solution)/shard_map/all_gather | solution.py:212
  114.3 197.7 %reduce-scatter.16.cloned.1.call-start = ((), (), s32[]{:S(2)}) async-start(), calls=%async_computation.11 | async-start | bytes 5013504
  165.2 264.0 %copy-start.76 = (f32[256]{0:T(256)}, f32[256]{0:T(256)S(1)}, u32[]{:S(2)}) copy-start(f32[256]{0:T(256)S(1)} %add_rsqrt_fusion.2) | copy-start | bytes 3076
  165.2 264.0 %copy-start.80 = (f32[256]{0:T(256)}, f32[256]{0:T(256)S(1)}, u32[]{:S(2)}) copy-start(f32[256]{0:T(256)S(1)} %add_rsqrt_fusion) | copy-start | bytes 3076
  237.7 74.3 %copy-start.59 = (f32[48,1536]{1,0:T(8,128)S(1)}, f32[48,1536]{1,0:T(8,128)}, u32[]{:S(2)}) copy-start(f32[48,1536]{1,0:T(8,128)} %param.34) | copy-start | bytes 884740
  237.8 118.5 %all-gather.11.cloned.1.call-start = ((), (), s32[]{:S(2)}) async-start(), calls=%async_computation.7 | async-start | bytes 2506752 | tf_op jit(solution)/shard_map/all_gather | solution.py:213
  314.3 112.2 %all-reduce.11.cloned.1.call-start = ((), (), s32[]{:S(2)}) async-start(), calls=%async_computation.14 | async-start | bytes 3145728 | tf_op jit(solution)/shard_map/psum | solution.py:126
  356.3 6.3 slice-start.6
  367.5 191.6 %all-reduce.9.cloned.1.call-start = ((), (), s32[]{:S(2)}) async-start(), calls=%async_computation.13 | async-start | bytes 3145728 | tf_op jit(solution)/shard_map/psum | solution.py:175
  431.9 18.9 %slice-start.2 = ((s8[4718592]{0:T(1024)(128)(4,1)}), s8[524288]{0:T(1024)(128)(4,1)S(1)}, s32[]{:S(2)}) async-start(s8[4718592]{0:T(1024)(128)(4,1)} %bitcast.246), calls=%async_computation.18 | async-start | bytes 1048576
  435.1 15.7 %slice-start.3 = ((s8[4718592]{0:T(1024)(128)(4,1)}), s8[4194304]{0:T(1024)(128)(4,1)S(1)}, s32[]{:S(2)}) async-start(s8[4718592]{0:T(1024)(128)(4,1)} %bitcast.246), calls=%async_computation.19 | async-start | bytes 8388608
  440.3 30.7 %collective-permute-start.10 = (bf16[256,6,64]{0,2,1:T(8,128)(2,1)}, bf16[256,6,64]{0,2,1:T(8,128)(2,1)}, u32[]{:S(2)}, u32[]{:S(2)}) collective-permute-start(bf16[256,6,64]{0,2,1:T(8,128)(2,1)} %get-tuple-element.167), channel_id=1, source_target_pairs={{1,0},{2,1},{3,2},{4,3},{5,4},{6,5},{7,6},{8,7},{9,8},{10,9},{11,1... | collective-permute-start | bytes 589832 | tf_op jit(solution)/shard_map/ppermute | solution.py:19
  441.6 30.7 %collective-permute-start.11 = (bf16[256,6,64]{0,2,1:T(8,128)(2,1)}, bf16[256,6,64]{0,2,1:T(8,128)(2,1)}, u32[]{:S(2)}, u32[]{:S(2)}) collective-permute-start(bf16[256,6,64]{0,2,1:T(8,128)(2,1)} %get-tuple-element.168), channel_id=1, source_target_pairs={{2,0},{3,1},{4,2},{5,3},{6,4},{7,5},{8,6},{9,7},{10,8},{11,9},{12,... | collective-permute-start | bytes 589832 | tf_op jit(solution)/shard_map/ppermute | solution.py:19
  442.9 7.9 copy-start.50
  442.9 7.9 copy-start.71
  448.0 29.2 %collective-permute-start.14 = (bf16[256,6,64]{0,2,1:T(8,128)(2,1)}, bf16[256,6,64]{0,2,1:T(8,128)(2,1)}, u32[]{:S(2)}, u32[]{:S(2)}) collective-permute-start(bf16[256,6,64]{0,2,1:T(8,128)(2,1)} %get-tuple-element.171), channel_id=1, source_target_pairs={{1,0},{2,1},{3,2},{4,3},{5,4},{6,5},{7,6},{8,7},{9,8},{10,9},{11,1... | collective-permute-start | bytes 589832 | tf_op jit(solution)/shard_map/ppermute | solution.py:19
  449.3 29.2 %collective-permute-start.15 = (bf16[256,6,64]{0,2,1:T(8,128)(2,1)}, bf16[256,6,64]{0,2,1:T(8,128)(2,1)}, u32[]{:S(2)}, u32[]{:S(2)}) collective-permute-start(bf16[256,6,64]{0,2,1:T(8,128)(2,1)} %get-tuple-element.172), channel_id=1, source_target_pairs={{2,0},{3,1},{4,2},{5,3},{6,4},{7,5},{8,6},{9,7},{10,8},{11,9},{12,... | collective-permute-start | bytes 589832 | tf_op jit(solution)/shard_map/ppermute | solution.py:19
  455.8 26.3 %collective-permute-start.12 = (bf16[256,6,64]{0,2,1:T(8,128)(2,1)}, bf16[256,6,64]{0,2,1:T(8,128)(2,1)}, u32[]{:S(2)}, u32[]{:S(2)}) collective-permute-start(bf16[256,6,64]{0,2,1:T(8,128)(2,1)} %get-tuple-element.169), channel_id=1, source_target_pairs={{1,0},{2,1},{3,2},{4,3},{5,4},{6,5},{7,6},{8,7},{9,8},{10,9},{11,1... | collective-permute-start | bytes 589832 | tf_op jit(solution)/shard_map/ppermute | solution.py:19
  471.0 12.5 %collective-permute-start.13 = (bf16[256,6,64]{0,2,1:T(8,128)(2,1)}, bf16[256,6,64]{0,2,1:T(8,128)(2,1)}, u32[]{:S(2)}, u32[]{:S(2)}) collective-permute-start(bf16[256,6,64]{0,2,1:T(8,128)(2,1)} %get-tuple-element.170), channel_id=1, source_target_pairs={{2,0},{3,1},{4,2},{5,3},{6,4},{7,5},{8,6},{9,7},{10,8},{11,9},{12,... | collective-permute-start | bytes 589832 | tf_op jit(solution)/shard_map/ppermute | solution.py:19
  472.3 11.2 %collective-permute-start.8 = (bf16[256,6,64]{0,2,1:T(8,128)(2,1)}, bf16[256,6,64]{0,2,1:T(8,128)(2,1)}, u32[]{:S(2)}, u32[]{:S(2)}) collective-permute-start(bf16[256,6,64]{0,2,1:T(8,128)(2,1)} %get-tuple-element.165), channel_id=1, source_target_pairs={{1,0},{2,1},{3,2},{4,3},{5,4},{6,5},{7,6},{8,7},{9,8},{10,9},{11,1... | collective-permute-start | bytes 589832 | tf_op jit(solution)/shard_map/ppermute | solution.py:19
  477.2 13.8 %collective-permute-start.9 = (bf16[256,6,64]{0,2,1:T(8,128)(2,1)}, bf16[256,6,64]{0,2,1:T(8,128)(2,1)}, u32[]{:S(2)}, u32[]{:S(2)}) collective-permute-start(bf16[256,6,64]{0,2,1:T(8,128)(2,1)} %get-tuple-element.166), channel_id=1, source_target_pairs={{2,0},{3,1},{4,2},{5,3},{6,4},{7,5},{8,6},{9,7},{10,8},{11,9},{12,... | collective-permute-start | bytes 589832 | tf_op jit(solution)/shard_map/ppermute | solution.py:19
  503.5 118.0 %reduce-scatter.12.cloned.1.call-start = ((), (), s32[]{:S(2)}) async-start(), calls=%async_computation.9 | async-start | bytes 1253376 | tf_op jit(solution)/shard_map/reduce_scatter | solution.py:221
  506.5 174.1 %reduce-scatter.18.cloned.1.call-start = ((), (), s32[]{:S(2)}) async-start(), calls=%async_computation.12 | async-start | bytes 417792
  508.4 50.6 %copy-start.85 = (f32[256]{0:T(256)S(1)}, f32[256]{0:T(256)}, u32[]{:S(2)}) copy-start(f32[256]{0:T(256)} %copy-done.84) | copy-start | bytes 3076
  512.0 51.9 %copy-start.51 = (bf16[256,1,384]{2,0,1:T(8,128)(2,1)S(1)}, bf16[256,1,384]{2,0,1:T(8,128)(2,1)}, u32[]{:S(2)}) copy-start(bf16[256,1,384]{2,0,1:T(8,128)(2,1)} %copy.164) | copy-start | bytes 589828
  512.0 51.9 %copy-start.52 = (bf16[256,1,384]{2,0,1:T(8,128)(2,1)S(1)}, bf16[256,1,384]{2,0,1:T(8,128)(2,1)}, u32[]{:S(2)}) copy-start(bf16[256,1,384]{2,0,1:T(8,128)(2,1)} %copy.166) | copy-start | bytes 589828
  563.8 188.2 %reduce-scatter.10.cloned.1.call-start = ((), (), s32[]{:S(2)}) async-start(), calls=%async_computation.8 | async-start | bytes 3760128 | tf_op jit(solution)/shard_map/reduce_scatter | solution.py:220
  568.7 297.5 %reduce-scatter.14.cloned.1.call-start = ((), (), s32[]{:S(2)}) async-start(), calls=%async_computation.10 | async-start | bytes 10027008 | tf_op jit(solution)/shard_map/reduce_scatter | solution.py:222
  582.9 38.6 %copy-start.60 = (f32[48,384]{1,0:T(8,128)S(1)}, f32[48,384]{1,0:T(8,128)}, u32[]{:S(2)}) copy-start(f32[48,384]{1,0:T(8,128)} %param.22) | copy-start | bytes 221188
  582.9 38.6 %copy-start.78 = (f32[48,384]{1,0:T(8,128)S(1)}, f32[48,384]{1,0:T(8,128)}, u32[]{:S(2)}) copy-start(f32[48,384]{1,0:T(8,128)} %param.32) | copy-start | bytes 221188
  582.9 38.6 %copy-start.79 = (f32[48,384]{1,0:T(8,128)S(1)}, f32[48,384]{1,0:T(8,128)}, u32[]{:S(2)}) copy-start(f32[48,384]{1,0:T(8,128)} %param.27) | copy-start | bytes 221188
  582.9 98.5 %copy-start.91 = (f32[48,2]{0,1:T(2,128)S(1)}, f32[48,2]{0,1:T(2,128)}, u32[]{:S(2)}) copy-start(f32[48,2]{0,1:T(2,128)} %param.25) | copy-start | bytes 1156
  582.9 98.5 %copy-start.92 = (f32[48,2]{0,1:T(2,128)S(1)}, f32[48,2]{0,1:T(2,128)}, u32[]{:S(2)}) copy-start(f32[48,2]{0,1:T(2,128)} %param.35) | copy-start | bytes 1156
  583.0 98.5 %copy-start.93 = (f32[48,2]{0,1:T(2,128)S(1)}, f32[48,2]{0,1:T(2,128)}, u32[]{:S(2)}) copy-start(f32[48,2]{0,1:T(2,128)} %param.30) | copy-start | bytes 1156
  583.0 169.1 %copy-start.28 = (f32[48,3,384]{2,0,1:T(8,128)S(1)}, f32[48,3,384]{2,0,1:T(8,128)}, u32[]{:S(2)}) copy-start(f32[48,3,384]{2,0,1:T(8,128)} %param.21) | copy-start | bytes 663556
  583.0 169.1 %copy-start.63 = (f32[48,3,384]{2,0,1:T(8,128)S(1)}, f32[48,3,384]{2,0,1:T(8,128)}, u32[]{:S(2)}) copy-start(f32[48,3,384]{2,0,1:T(8,128)} %param.31) | copy-start | bytes 663556
  583.0 169.1 %copy-start.64 = (f32[48,3,384]{2,0,1:T(8,128)S(1)}, f32[48,3,384]{2,0,1:T(8,128)}, u32[]{:S(2)}) copy-start(f32[48,3,384]{2,0,1:T(8,128)} %param.26) | copy-start | bytes 663556
  584.2 282.0 %copy-start.19 = (f32[48,2,1536]{2,1,0:T(2,128)S(1)}, f32[48,2,1536]{2,1,0:T(2,128)}, u32[]{:S(2)}) copy-start(f32[48,2,1536]{2,1,0:T(2,128)} %param.23) | copy-start | bytes 1769476
  584.3 282.0 %copy-start.57 = (f32[48,2,1536]{2,1,0:T(2,128)S(1)}, f32[48,2,1536]{2,1,0:T(2,128)}, u32[]{:S(2)}) copy-start(f32[48,2,1536]{2,1,0:T(2,128)} %param.33) | copy-start | bytes 1769476
  584.3 282.0 %copy-start.58 = (f32[48,2,1536]{2,1,0:T(2,128)S(1)}, f32[48,2,1536]{2,1,0:T(2,128)}, u32[]{:S(2)}) copy-start(f32[48,2,1536]{2,1,0:T(2,128)} %param.28) | copy-start | bytes 1769476
  681.5 186.3 %copy-start.90 = (f32[48,2]{0,1:T(2,128)}, f32[48,2]{0,1:T(2,128)S(1)}, u32[]{:S(2)}) copy-start(f32[48,2]{0,1:T(2,128)S(1)} %copy.192) | copy-start | bytes 1156
  (66 other events, 171.1 us)
Sparse Core Ops, SparseCore 0:
  10.9 45.0 all-gather.6
  113.5 49.9 all-reduce.12
  166.4 53.1 all-gather.8
  237.9 74.1 reduce-scatter.15
  314.8 41.4 all-gather.10
  367.6 58.9 all-reduce.10
  503.6 55.4 all-reduce.8
  563.2 58.1 reduce-scatter.11
  625.5 55.0 reduce-scatter.17
  684.9 67.0 reduce-scatter.9
  756.2 110.0 reduce-scatter.13
